TPU v7x, 32 devices: a whole 2x2x4 slice. The times are simulated.
32 devices in a mesh: cube: 8 (over z, y), blk: 4 (over x, core).
Axes of the slice: x: 2, y: 2, z: 4, core: 2. Of those that a mesh axis runs over, the one named last changes fastest.
Arguments:
- rhs_root: bfloat16 [1, 10240, 128], P(None, 'blk'), may hold values from -6 to 6
- rhs_mid: bfloat16 [2, 10240, 128], P(None, 'blk'), may hold values from -6 to 6
- rhs_leaf: bfloat16 [4, 10240, 128], P(None, 'blk'), may hold values from -6 to 6
- pivot_root: bfloat16 [2, 10240, 10240], P(None, 'cube', 'blk'), may hold values from -0.0625 to 0.0625
- pivot_mid: bfloat16 [2, 20480, 10240], P(None, 'cube', 'blk'), may hold values from -0.0625 to 0.0625
- pivot_leaf: bfloat16 [2, 40960, 10240], P(None, 'cube', 'blk'), may hold values from -0.0625 to 0.0625
- coupling_mid: bfloat16 [2, 2560, 10240], P(None, 'cube', 'blk'), may hold values from -0.0625 to 0.0625
- coupling_leaf: bfloat16 [2, 5120, 10240], P(None, 'cube', 'blk'), may hold values from -0.0625 to 0.0625
- front_blocks: int32 [7], replicated, may hold values from 40 to 80, as said below
- child_map: int32 [6, 10], replicated, may hold values from 0 to 79
Outputs:
- solution_root: bfloat16 [4, 2560, 128], P('blk', 'cube')
- solution_mid: bfloat16 [4, 5120, 128], P('blk', 'cube')
- solution_leaf: bfloat16 [4, 10240, 128], P('blk', 'cube')
Inputs may be any that keep to these rules, and one draw needn't show every extreme that they name: `front_blocks`: entry 0 is the root, entries 1 and 2 the level-1 fronts, 3 to 6 the level-2 fronts; at least one front is full in every draw. `child_map`: rows 0 and 1 belong to the level-1 fronts, row 2 + q to level-2 front q; targets may repeat within and across children.
All inputs are finite; a program needn't handle non-finite values.
Results may differ from a plain program's by a relative error of at most 0.013.
Values may be sent and summed in bfloat16 or wider, within the bound.
A program may use at most 192 MiB of HBM per device.

v0:
```python
import jax
import jax.numpy as jnp
from jax import lax
from jax.sharding import PartitionSpec as P

SEPARATOR = 10240
BLOCK_ROWS = 128


def swapped(value, axis, distance):
    return lax.ppermute(value, axis, [(i, i ^ 1 << distance) for i in range(lax.axis_size(axis))])


def rotate_parts(vec):
    half = vec.shape[1] // 2
    return jnp.concatenate([-vec[:, half:], vec[:, :half]], axis=1)


def complex_apply(matrix, vec):
    first = jnp.dot(matrix[0], vec, preferred_element_type=jnp.float32)
    second = jnp.dot(matrix[1], rotate_parts(vec), preferred_element_type=jnp.float32)
    return first + second


def complex_apply_t(matrix, vec):
    dims = (((0,), (0,)), ((), ()))
    first = lax.dot_general(matrix[0], vec, dims, preferred_element_type=jnp.float32)
    second = lax.dot_general(matrix[1], rotate_parts(vec), dims, preferred_element_type=jnp.float32)
    return first + second


def bit_set(cube_at, bit):
    return cube_at >> bit & 1 == 1


def gather_bits(piece, count, cube_at):
    for bit in range(count):
        other = swapped(piece, "cube", bit)
        upper = bit_set(cube_at, bit)
        piece = jnp.where(
            upper, jnp.concatenate([other, piece], 0), jnp.concatenate([piece, other], 0)
        )
    return piece


def swap_sum(value, bit):
    return swapped(value.astype(jnp.bfloat16), "cube", bit).astype(value.dtype)


def halve_bits(total, count, cube_at):
    for bit in reversed(range(count)):
        rows = total.shape[0] // 2
        lower = total[:rows]
        higher = total[rows:]
        upper = bit_set(cube_at, bit)
        sent = jnp.where(upper, lower, higher)
        kept = jnp.where(upper, higher, lower)
        total = kept + swap_sum(sent, bit)
    return total


def blk_total(value):
    return lax.psum(value, "blk")


def row_mask(start, count, limit):
    rows = start + jnp.arange(count, dtype=jnp.int32)
    return (rows < limit).astype(jnp.float32)[:, None]


def extend_add(gathered, targets, first_block, slice_blocks):
    blocks = gathered.reshape(targets.shape[0], BLOCK_ROWS, gathered.shape[1])
    slots = jnp.arange(slice_blocks, dtype=jnp.int32)
    placing = (targets[None, :] - first_block == slots[:, None]).astype(jnp.bfloat16)
    summed = jnp.einsum("ti,ird->trd", placing, blocks, preferred_element_type=jnp.float32)
    return summed.reshape(slice_blocks * BLOCK_ROWS, gathered.shape[1])


def pick_rows(parent_slice, targets, rows, first_row):
    block_of = rows // BLOCK_ROWS
    table = (block_of[:, None] == jnp.arange(targets.shape[0], dtype=jnp.int32)[None, :]).astype(
        jnp.int32
    )
    target_block = jnp.sum(table * targets[None, :], axis=1)
    where_row = target_block * BLOCK_ROWS + rows % BLOCK_ROWS - first_row
    inside = (where_row >= 0) & (where_row < parent_slice.shape[0])
    values = parent_slice[jnp.clip(where_row, 0, parent_slice.shape[0] - 1)].astype(jnp.float32)
    return jnp.where(inside[:, None], values, 0.0)


def forward_front(pivot, coupling, gathered, column_mask, solved_mask):
    masked = (column_mask * gathered).astype(jnp.bfloat16)
    own_rows = pivot.shape[1]
    if coupling is None:
        sums = blk_total(complex_apply(pivot, masked))
        return ((solved_mask * sums).astype(jnp.bfloat16), None)
    both = jnp.concatenate([complex_apply(pivot, masked), complex_apply(coupling, masked)], 0)
    sums = blk_total(both)
    solved = (solved_mask * sums[:own_rows]).astype(jnp.bfloat16)
    return (solved, sums[own_rows:].astype(jnp.bfloat16))


def per_device(
    rhs_root,
    rhs_mid,
    rhs_leaf,
    pivot_root,
    pivot_mid,
    pivot_leaf,
    coupling_mid,
    coupling_leaf,
    front_blocks,
    child_map,
):
    cube_n = lax.axis_size("cube")
    blk_n = lax.axis_size("blk")
    cube_at = lax.axis_index("cube")
    blk_at = lax.axis_index("blk")
    slice_rows = SEPARATOR // blk_n
    slice_blocks = slice_rows // BLOCK_ROWS
    first_row = blk_at * slice_rows
    first_block = blk_at * slice_blocks
    group_mid = cube_n // 2
    group_leaf = cube_n // 4
    bits_root = cube_n.bit_length() - 1
    bits_mid = bits_root - 1
    bits_leaf = bits_root - 2
    front_mid = cube_at // group_mid
    place_mid = cube_at % group_mid
    front_leaf = cube_at // group_leaf
    place_leaf = cube_at % group_leaf
    size_root = front_blocks[0] * BLOCK_ROWS
    size_mid = front_blocks[1 + front_mid] * BLOCK_ROWS
    size_leaf = front_blocks[3 + front_leaf] * BLOCK_ROWS
    column_leaf = row_mask(first_row, slice_rows, size_leaf)
    column_mid = row_mask(first_row, slice_rows, size_mid)
    column_root = row_mask(first_row, slice_rows, size_root)
    own_leaf = pivot_leaf.shape[1]
    gathered = lax.dynamic_index_in_dim(rhs_leaf, front_leaf, 0, keepdims=False).astype(jnp.float32)
    solved_leaf, update_leaf = forward_front(
        pivot_leaf,
        coupling_leaf,
        gathered,
        column_leaf,
        row_mask(place_leaf * own_leaf, own_leaf, size_leaf),
    )
    own_mid = pivot_mid.shape[1]
    arrived = gather_bits(update_leaf, bits_mid, cube_at)
    targets = lax.dynamic_slice_in_dim(child_map, 2 + 2 * front_mid, 2, 0).reshape(-1)
    gathered = lax.dynamic_index_in_dim(rhs_mid, front_mid, 0, keepdims=False).astype(jnp.float32)
    gathered = gathered - extend_add(arrived, targets, first_block, slice_blocks)
    solved_mid, update_mid = forward_front(
        pivot_mid,
        coupling_mid,
        gathered,
        column_mid,
        row_mask(place_mid * own_mid, own_mid, size_mid),
    )
    own_root = pivot_root.shape[1]
    arrived = gather_bits(update_mid, bits_root, cube_at)
    targets = child_map[0:2].reshape(-1)
    gathered = rhs_root[0].astype(jnp.float32) - extend_add(
        arrived, targets, first_block, slice_blocks
    )
    solved_root, unused = forward_front(
        pivot_root, None, gathered, column_root, row_mask(cube_at * own_root, own_root, size_root)
    )
    total = lax.psum(complex_apply_t(pivot_root, solved_root), "cube")
    full_root = (column_root * total).astype(jnp.bfloat16)
    piece_root = slice_rows // cube_n
    answer_root = lax.dynamic_slice_in_dim(full_root, cube_at * piece_root, piece_root, 0)
    update_rows_mid = coupling_mid.shape[1]
    rows = place_mid * update_rows_mid + jnp.arange(update_rows_mid, dtype=jnp.int32)
    targets = lax.dynamic_slice_in_dim(child_map, front_mid, 1, 0).reshape(-1)
    pulled = blk_total(pick_rows(full_root, targets, rows, first_row)).astype(jnp.bfloat16)
    term = complex_apply_t(pivot_mid, solved_mid) - complex_apply_t(coupling_mid, pulled)
    piece_mid = slice_rows // group_mid
    share = halve_bits(term, bits_mid, cube_at)
    answer_mid = (row_mask(first_row + place_mid * piece_mid, piece_mid, size_mid) * share).astype(
        jnp.bfloat16
    )
    full_mid = gather_bits(answer_mid, bits_mid, cube_at)
    update_rows_leaf = coupling_leaf.shape[1]
    rows = place_leaf * update_rows_leaf + jnp.arange(update_rows_leaf, dtype=jnp.int32)
    targets = lax.dynamic_slice_in_dim(child_map, 2 + front_leaf, 1, 0).reshape(-1)
    pulled = blk_total(pick_rows(full_mid, targets, rows, first_row)).astype(jnp.bfloat16)
    term = complex_apply_t(pivot_leaf, solved_leaf) - complex_apply_t(coupling_leaf, pulled)
    piece_leaf = slice_rows // group_leaf
    share = halve_bits(term, bits_leaf, cube_at)
    answer_leaf = (
        row_mask(first_row + place_leaf * piece_leaf, piece_leaf, size_leaf) * share
    ).astype(jnp.bfloat16)
    return (answer_root[None], answer_mid[None], answer_leaf[None])


def solution(mesh):
    in_specs = (
        P(None, "blk", None),
        P(None, "blk", None),
        P(None, "blk", None),
        P(None, "cube", "blk"),
        P(None, "cube", "blk"),
        P(None, "cube", "blk"),
        P(None, "cube", "blk"),
        P(None, "cube", "blk"),
        P(),
        P(),
    )
    out_specs = (P("blk", "cube", None), P("blk", "cube", None), P("blk", "cube", None))
    return jax.shard_map(
        per_device, mesh=mesh, in_specs=in_specs, out_specs=out_specs, check_vma=False
    )
```

profile of v0, /device:TPU:0, one launch (start us, length us, event | category | flops | bytes accessed | tf_op | source)
XLA Modules:
  0.0 470.1 jit_solution(2196238573120029285)
XLA Ops:
  11.7 3.4 fusion.65
  18.0 15.5 %fusion.2 = f32[128,5120]{1,0:T(8,128)} fusion(bf16[2,5120,2560]{2,1,0:T(8,128)(2,1)} %param.15, bf16[2560,64]{1,0:T(8,128)(2,1)S(1)} %get-tuple-element.24, bf16[2560,64]{1,0:T(8,128)(2,1)S(1)} %get-tuple-element.23), kind=kOutput, calls=%fused_computation.4 | convolution fusion | flops 3356753920 | bytes 29491200 | tf_op jit(solution)/shard_map/dot_general | solution.py:21
  33.6 15.2 %fusion.35 = f32[5120,128]{0,1:T(8,128)S(1)} fusion(f32[128,5120]{1,0:T(8,128)} %fusion.2, bf16[2,5120,2560]{2,1,0:T(8,128)(2,1)} %param.15, f32[2560]{0:T(1024)S(1)} %get-tuple-element.43, bf16[4,2560,128]{2,1,0:T(8,128)(2,1)} %param.12, s32[]{:T(128)S(6)} %select_n.217), kind=kOutput, calls=%fused_computation.35 | convolution fusion | flops 3357081600 | bytes 32122884 | tf_op jit(solution)/shard_map/dot_general | solution.py:20
  52.1 66.6 %all-reduce.7.cloned.1.call-done = f32[5760,128]{0,1:T(8,128)} async-done(((f32[5760,128]{0,1:T(8,128)}), f32[5760,128]{0,1:T(8,128)}) %all-reduce.7.cloned.1.call-update) | async-done | bytes 2949136 | tf_op jit(solution)/shard_map/psum | solution.py:63
  127.2 6.7 %collective-permute-done.1 = bf16[1280,128]{0,1:T(8,128)(2,1)S(1)} collective-permute-done((bf16[1280,128]{0,1:T(8,128)(2,1)S(1)}, bf16[1280,128]{0,1:T(8,128)(2,1)S(1)}, u32[]{:S(2)}, u32[]{:S(2)}) %collective-permute-start.1) | collective-permute-done | bytes 327712 | tf_op jit(solution)/shard_map/ppermute | solution.py:11
  139.8 7.9 %fusion.14 = f32[128,2560]{1,0:T(8,128)S(1)} fusion(bf16[2,2560,2560]{2,1,0:T(8,128)(2,1)} %param.14, bf16[2560,64]{1,0:T(8,128)(2,1)S(1)} %get-tuple-element.22, bf16[2560,64]{1,0:T(8,128)(2,1)S(1)} %get-tuple-element.21), kind=kOutput, calls=%fused_computation.16 | convolution fusion | flops 1679032320 | bytes 15073280 | tf_op jit(solution)/shard_map/dot_general | solution.py:21
  147.7 7.4 %fusion.58 = f32[2560,128]{0,1:T(8,128)S(1)} fusion(f32[128,2560]{1,0:T(8,128)S(1)} %fusion.14, bf16[2560,128]{1,0:T(8,128)(2,1)S(1)} %bitcast.160, bf16[2,2560,2560]{2,1,0:T(8,128)(2,1)} %param.14), kind=kOutput, calls=%fused_computation.50 | convolution fusion | flops 1678049280 | bytes 16384000 | tf_op jit(solution)/shard_map/dot_general | solution.py:20
  159.8 40.0 %all-reduce.9.cloned.1.call-done = f32[2880,128]{0,1:T(8,128)} async-done(((f32[2880,128]{0,1:T(8,128)}), f32[2880,128]{0,1:T(8,128)}) %all-reduce.9.cloned.1.call-update) | async-done | bytes 1474576 | tf_op jit(solution)/shard_map/psum | solution.py:63
  217.1 11.0 %collective-permute-done.4 = bf16[1280,128]{0,1:T(8,128)(2,1)S(1)} collective-permute-done((bf16[1280,128]{0,1:T(8,128)(2,1)S(1)}, bf16[1280,128]{0,1:T(8,128)(2,1)S(1)}, u32[]{:S(2)}, u32[]{:S(2)}) %collective-permute-start.4) | collective-permute-done | bytes 327712 | tf_op jit(solution)/shard_map/ppermute | solution.py:11
  231.8 5.1 %fusion.26 = f32[128,1280]{1,0:T(8,128)S(1)} fusion(bf16[2,1280,2560]{2,1,0:T(8,128)(2,1)} %param.13, bf16[2560,64]{0,1:T(8,128)(2,1)S(1)} %get-tuple-element.20, bf16[2560,64]{0,1:T(8,128)(2,1)S(1)} %get-tuple-element.19), kind=kOutput, calls=%fused_computation.28 | convolution fusion | flops 840171520 | bytes 7864320 | tf_op jit(solution)/shard_map/dot_general | solution.py:21
  237.0 6.1 %fusion.79 = f32[1280,128]{0,1:T(8,128)} fusion(f32[128,1280]{1,0:T(8,128)S(1)} %fusion.26, bf16[2560,128]{1,0:T(8,128)(2,1)S(1)} %bitcast.162, bf16[2,1280,2560]{2,1,0:T(8,128)(2,1)} %param.13), kind=kOutput, calls=%fused_computation.67 | convolution fusion | flops 839024640 | bytes 8519680 | tf_op jit(solution)/shard_map/dot_general | solution.py:20
  243.2 34.1 %all-reduce.11.cloned.1.call-done = f32[1280,128]{0,1:T(8,128)} async-done(((f32[1280,128]{0,1:T(8,128)}), f32[1280,128]{0,1:T(8,128)}) %all-reduce.11.cloned.1.call-update) | async-done | bytes 655376 | tf_op jit(solution)/shard_map/psum | solution.py:63
  278.5 3.9 fusion.24
  282.3 5.0 %fusion.49 = f32[2560,128]{0,1:T(8,128)} fusion(f32[128,2560]{1,0:T(8,128)S(1)} %fusion.24, bf16[1280,128]{0,1:T(8,128)(2,1)S(1)} %multiply_convert_fusion.2, bf16[2,1280,2560]{2,1,0:T(8,128)(2,1)} %param.13), kind=kOutput, calls=%fused_computation.47 | convolution fusion | flops 839188480 | bytes 9502720 | tf_op jit(solution)/shard_map/dot_general | solution.py:27
  287.4 5.8 %fusion.12 = f32[128,2560]{1,0:T(8,128)S(1)} fusion(bf16[2,2560,2560]{2,1,0:T(8,128)(2,1)} %param.14, bf16[2560,64]{0,1:T(8,128)(2,1)S(1)} %get-tuple-element.18, bf16[2560,64]{0,1:T(8,128)(2,1)S(1)} %get-tuple-element.17), kind=kOutput, calls=%fused_computation.14 | convolution fusion | flops 1679032320 | bytes 15073280 | tf_op jit(solution)/shard_map/dot_general | solution.py:28
  293.2 7.7 %fusion.61 = f32[128,2560]{1,0:T(8,128)} fusion(f32[128,2560]{1,0:T(8,128)S(1)} %fusion.12, bf16[2560,128]{0,1:T(8,128)(2,1)S(1)} %copy-done.4, bf16[2,2560,2560]{2,1,0:T(8,128)(2,1)} %param.14), kind=kOutput, calls=%fused_computation.51 | convolution fusion | flops 1678049280 | bytes 16384000 | tf_op jit(solution)/shard_map/dot_general | solution.py:27
  300.8 70.3 %all-reduce.13.cloned.1.call-done = f32[2560,128]{0,1:T(8,128)} async-done(((f32[2560,128]{0,1:T(8,128)}), f32[2560,128]{0,1:T(8,128)}) %all-reduce.13.cloned.1.call-update) | async-done | bytes 1310736 | tf_op jit(solution)/shard_map/psum | solution.py:168
  378.1 13.4 %all-reduce.14 = bf16[320,128]{1,0:T(8,128)(2,1)S(1)} all-reduce(f32[320,128]{1,0:T(8,128)S(1)} %convert_select_fusion.1), channel_id=1, replica_groups=mesh['cube'=8,'blk'=4] {'blk'}, use_global_device_ids=true, to_apply=%region_5.6 | all-reduce | flops 40960 | bytes 245760 | tf_op jit(solution)/shard_map/psum | solution.py:63
  395.0 7.4 %collective-permute-done.5 = bf16[1280,128]{0,1:T(8,128)(2,1)S(1)} collective-permute-done((bf16[1280,128]{0,1:T(8,128)(2,1)S(1)}, bf16[1280,128]{0,1:T(8,128)(2,1)S(1)}, u32[]{:S(2)}, u32[]{:S(2)}) %collective-permute-start.5) | collective-permute-done | bytes 327712 | tf_op jit(solution)/shard_map/ppermute | solution.py:11
  404.1 4.0 collective-permute-done.6
  409.7 10.3 %fusion = f32[128,2560]{1,0:T(8,128)S(1)} fusion(bf16[2,5120,2560]{2,1,0:T(8,128)(2,1)} %param.15, bf16[5120,64]{0,1:T(8,128)(2,1)S(1)} %get-tuple-element.16, bf16[5120,64]{0,1:T(8,128)(2,1)S(1)} %get-tuple-element.15), kind=kOutput, calls=%fused_computation.2 | convolution fusion | flops 3358064640 | bytes 28835840 | tf_op jit(solution)/shard_map/dot_general | solution.py:28
  421.4 10.5 %fusion.52 = f32[128,2560]{1,0:T(8,128)S(1)} fusion(f32[128,2560]{1,0:T(8,128)S(1)} %fusion, bf16[5120,128]{0,1:T(8,128)(2,1)S(1)} %fusion.75, bf16[2,5120,2560]{2,1,0:T(8,128)(2,1)} %param.15), kind=kOutput, calls=%fused_computation.48 | convolution fusion | flops 3355770880 | bytes 30146560 | tf_op jit(solution)/shard_map/dot_general | solution.py:27
  434.7 14.0 %all-reduce.15 = bf16[640,128]{1,0:T(8,128)(2,1)S(1)} all-reduce(f32[640,128]{1,0:T(8,128)S(1)} %convert_select_fusion), channel_id=1, replica_groups=mesh['cube'=8,'blk'=4] {'blk'}, use_global_device_ids=true, to_apply=%region_7.8 | all-reduce | flops 81920 | bytes 491520 | tf_op jit(solution)/shard_map/psum | solution.py:63
  457.4 4.9 %collective-permute-done.9 = bf16[1280,128]{0,1:T(8,128)(2,1)S(1)} collective-permute-done((bf16[1280,128]{0,1:T(8,128)(2,1)S(1)}, bf16[1280,128]{0,1:T(8,128)(2,1)S(1)}, u32[]{:S(2)}, u32[]{:S(2)}) %collective-permute-start.9) | collective-permute-done | bytes 327712 | tf_op jit(solution)/shard_map/ppermute | solution.py:11
  (151 shorter events, 77.3 us)
Async XLA Ops:
  7.2 111.5 %all-reduce.7.cloned.1.call-start = ((), (), s32[]{:S(2)}) async-start(), calls=%async_computation | async-start | bytes 5898240 | tf_op jit(solution)/shard_map/psum | solution.py:63
  50.5 76.5 %copy-start.6 = (bf16[2,2560,128]{2,1,0:T(8,128)(2,1)S(1)}, bf16[2,2560,128]{2,1,0:T(8,128)(2,1)}, u32[]{:S(2)}) copy-start(bf16[2,2560,128]{2,1,0:T(8,128)(2,1)} %param.11) | copy-start | bytes 3932164
  50.6 149.2 %all-reduce.9.cloned.1.call-start = ((), (), s32[]{:S(2)}) async-start(), calls=%async_computation.1 | async-start | bytes 3014656 | tf_op jit(solution)/shard_map/psum | solution.py:63
  119.7 5.7 %collective-permute-start = (bf16[640,128]{0,1:T(8,128)(2,1)S(1)}, bf16[640,128]{0,1:T(8,128)(2,1)S(1)}, u32[]{:S(2)}, u32[]{:S(2)}) collective-permute-start(bf16[640,128]{0,1:T(8,128)(2,1)S(1)} %slice.339), channel_id=1, source_target_pairs={{0,4},{4,0},{8,12},{12,8},{16,20},{20,16},{24,28},{28,24},{1,5},{5... | collective-permute-start | bytes 491528 | tf_op jit(solution)/shard_map/ppermute | solution.py:11
  125.5 8.4 %collective-permute-start.1 = (bf16[1280,128]{0,1:T(8,128)(2,1)S(1)}, bf16[1280,128]{0,1:T(8,128)(2,1)S(1)}, u32[]{:S(2)}, u32[]{:S(2)}) collective-permute-start(bf16[1280,128]{0,1:T(8,128)(2,1)S(1)} %maximum_select_fusion.3), channel_id=1, source_target_pairs={{0,8},{4,12},{8,0},{12,4},{16,24},{20,28},{24,16},{28,20},{1,9},{5... | collective-permute-start | bytes 983048 | tf_op jit(solution)/shard_map/ppermute | solution.py:11
  157.1 51.8 %copy-start.9 = (bf16[1,2560,128]{2,1,0:T(8,128)(2,1)S(1)}, bf16[1,2560,128]{2,1,0:T(8,128)(2,1)}, u32[]{:S(2)}) copy-start(bf16[1,2560,128]{2,1,0:T(8,128)(2,1)} %param.10) | copy-start | bytes 1966084
  157.2 120.1 %all-reduce.11.cloned.1.call-start = ((), (), s32[]{:S(2)}) async-start(), calls=%async_computation.2 | async-start | bytes 1310720 | tf_op jit(solution)/shard_map/psum | solution.py:63
  200.7 4.7 collective-permute-start.2
  206.2 5.6 %collective-permute-start.3 = (bf16[640,128]{0,1:T(8,128)(2,1)}, bf16[640,128]{0,1:T(8,128)(2,1)}, u32[]{:S(2)}, u32[]{:S(2)}) collective-permute-start(bf16[640,128]{0,1:T(8,128)(2,1)} %maximum_select_fusion.6), channel_id=1, source_target_pairs={{0,8},{4,12},{8,0},{12,4},{16,24},{20,28},{24,16},{28,20},{1,9},{5... | collective-permute-start | bytes 491528 | tf_op jit(solution)/shard_map/ppermute | solution.py:11
  209.2 6.3 %copy-start.5 = (f32[2880,128]{0,1:T(8,128)S(1)}, f32[2880,128]{0,1:T(8,128)}, u32[]{:S(2)}) copy-start(f32[2880,128]{0,1:T(8,128)} %all-reduce.9.cloned.1.call-done) | copy-start | bytes 4423684
  213.0 15.1 %collective-permute-start.4 = (bf16[1280,128]{0,1:T(8,128)(2,1)S(1)}, bf16[1280,128]{0,1:T(8,128)(2,1)S(1)}, u32[]{:S(2)}, u32[]{:S(2)}) collective-permute-start(bf16[1280,128]{0,1:T(8,128)(2,1)S(1)} %maximum_select_fusion.4), channel_id=1, source_target_pairs={{0,16},{4,20},{8,24},{12,28},{16,0},{20,4},{24,8},{28,12},{1,17},{... | collective-permute-start | bytes 983048 | tf_op jit(solution)/shard_map/ppermute | solution.py:11
  217.1 11.5 %copy-start.18 = (s32[20]{0:T(128)S(1)}, s32[20]{0:T(128)}, u32[]{:S(2)}) copy-start(s32[20]{0:T(128)} %sub.112) | copy-start | bytes 244
  231.8 5.1 %copy-start.10 = (bf16[20,128,128]{2,1,0:T(8,128)(2,1)S(1)}, bf16[20,128,128]{2,1,0:T(8,128)(2,1)}, u32[]{:S(2)}) copy-start(bf16[20,128,128]{2,1,0:T(8,128)(2,1)} %copy.75) | copy-start | bytes 1966084
  236.9 6.2 %copy-start.4 = (bf16[2560,128]{0,1:T(8,128)(2,1)S(1)}, bf16[2560,128]{0,1:T(8,128)(2,1)}, u32[]{:S(2)}) copy-start(bf16[2560,128]{0,1:T(8,128)(2,1)} %fusion.100) | copy-start | bytes 1966084
  243.1 34.2 %copy-start.12 = (f32[1280]{0:T(1024)S(1)}, f32[1280]{0:T(1024)}, u32[]{:S(2)}) copy-start(f32[1280]{0:T(1024)} %fusion.159) | copy-start | bytes 15364
  243.1 128.1 %all-reduce.13.cloned.1.call-start = ((), (), s32[]{:S(2)}) async-start(), calls=%async_computation.3 | async-start | bytes 2621440 | tf_op jit(solution)/shard_map/psum | solution.py:168
  300.8 74.9 %copy-start.14 = (s32[1024]{0:T(1024)S(1)}, s32[1024]{0:T(1024)}, u32[]{:S(2)}) copy-start(s32[1024]{0:T(1024)} %pad_clamp_fusion.1) | copy-start | bytes 12292
  371.1 20.5 %copy-start.2 = (bf16[2,320,2560]{2,1,0:T(8,128)(2,1)S(1)}, bf16[2,320,2560]{2,1,0:T(8,128)(2,1)}, u32[]{:S(2)}) copy-start(bf16[2,320,2560]{2,1,0:T(8,128)(2,1)} %param.16) | copy-start | bytes 9830404
  373.5 4.5 copy-start.17
  393.6 8.7 %collective-permute-start.5 = (bf16[1280,128]{0,1:T(8,128)(2,1)S(1)}, bf16[1280,128]{0,1:T(8,128)(2,1)S(1)}, u32[]{:S(2)}, u32[]{:S(2)}) collective-permute-start(bf16[1280,128]{0,1:T(8,128)(2,1)S(1)} %select_convert_fusion.1), channel_id=1, source_target_pairs={{0,8},{4,12},{8,0},{12,4},{16,24},{20,28},{24,16},{28,20},{1,9},{5... | collective-permute-start | bytes 983048 | tf_op jit(solution)/shard_map/ppermute | solution.py:11
  402.5 5.6 %collective-permute-start.6 = (bf16[640,128]{0,1:T(8,128)(2,1)S(1)}, bf16[640,128]{0,1:T(8,128)(2,1)S(1)}, u32[]{:S(2)}, u32[]{:S(2)}) collective-permute-start(bf16[640,128]{0,1:T(8,128)(2,1)S(1)} %select_convert_fusion.2), channel_id=1, source_target_pairs={{0,4},{4,0},{8,12},{12,8},{16,20},{20,16},{24,28},{28,24},{1,5},{5... | collective-permute-start | bytes 491528 | tf_op jit(solution)/shard_map/ppermute | solution.py:11
  408.2 11.9 %collective-permute-start.7 = (bf16[640,128]{0,1:T(8,128)(2,1)S(1)}, bf16[640,128]{0,1:T(8,128)(2,1)S(1)}, u32[]{:S(2)}, u32[]{:S(2)}) collective-permute-start(bf16[640,128]{0,1:T(8,128)(2,1)S(1)} %multiply_convert_fusion.3), channel_id=1, source_target_pairs={{0,4},{4,0},{8,12},{12,8},{16,20},{20,16},{24,28},{28,24},{1,5},{5... | collective-permute-start | bytes 491528 | tf_op jit(solution)/shard_map/ppermute | solution.py:11
  420.2 11.7 %collective-permute-start.8 = (bf16[1280,128]{0,1:T(8,128)(2,1)S(1)}, bf16[1280,128]{0,1:T(8,128)(2,1)S(1)}, u32[]{:S(2)}, u32[]{:S(2)}) collective-permute-start(bf16[1280,128]{0,1:T(8,128)(2,1)S(1)} %maximum_select_fusion.5), channel_id=1, source_target_pairs={{0,8},{4,12},{8,0},{12,4},{16,24},{20,28},{24,16},{28,20},{1,9},{5... | collective-permute-start | bytes 983048 | tf_op jit(solution)/shard_map/ppermute | solution.py:11
  454.3 8.0 %collective-permute-start.9 = (bf16[1280,128]{0,1:T(8,128)(2,1)S(1)}, bf16[1280,128]{0,1:T(8,128)(2,1)S(1)}, u32[]{:S(2)}, u32[]{:S(2)}) collective-permute-start(bf16[1280,128]{0,1:T(8,128)(2,1)S(1)} %select_convert_fusion), channel_id=1, source_target_pairs={{0,4},{4,0},{8,12},{12,8},{16,20},{20,16},{24,28},{28,24},{1,5},{5... | collective-permute-start | bytes 983048 | tf_op jit(solution)/shard_map/ppermute | solution.py:11
  (9 other events, 16.5 us)
Sparse Core Ops, SparseCore 0:
  50.7 67.9 all-reduce.6
  157.3 42.4 all-reduce.8
  243.2 34.0 all-reduce.10
  287.5 83.6 all-reduce.12
where the time goes:
time: 478 us; the launch traced here: 470 us
  waiting for transfers between devices  253 us (53%)
  matrix products  117 us (24%)
  blocking collectives  27.4 us (6%)
  local copies, waits for them, and re-layouts  22.2 us (5%)
  other arithmetic  19.3 us (4%)
  between operations  16.7 us (3%)
  starting transfers between devices  14.3 us (3%)
    psum x3, waiting for transfers between devices, blk_total(): return lax.psum(value, 'blk')  141 us
    psum x1, waiting for transfers between devices, per_device(): total = lax.psum(complex_apply_t(pivot_root, solved_root), 'cube')  70.3 us
    ppermute x10, waiting for transfers between devices, swapped(): lax.ppermute(value, axis, [(i, i ^ 1 << distance) for i in range(lax.axis...  42.2 us
    dot_general x5, matrix products, complex_apply(): jnp.dot(matrix[1], rotate_parts(vec), preferred_element_type=jnp.float32)  32.6 us
    dot_general x5, matrix products, complex_apply(): first = jnp.dot(matrix[0], vec, preferred_element_type=jnp.float32)  32 us
    psum x2, blocking collectives, blk_total(): return lax.psum(value, 'blk')  27.4 us
    dot_general x5, matrix products, complex_apply_t(): lax.dot_general(matrix[0], vec, dims, preferred_element_type=jnp.float32)  26.3 us
    dot_general x5, matrix products, complex_apply_t(): lax.dot_general(matrix[1], rotate_parts(vec), dims, preferred_element_typ...  23.4 us
  transfers between devices with their start and end apart: 14, of which 12 were waited for; matrix products, arithmetic and copies ran while one was open for 10% of the time, Pallas kernels for 0%

commit v1 on v0

--- a/solution.py
+++ b/solution.py
@@ -5,6 +5,11 @@
 
 SEPARATOR = 10240
 BLOCK_ROWS = 128
+
+
+def add_all(value, mesh_axis):
+    parts = lax.all_gather(value, mesh_axis)
+    return jnp.sum(parts, axis=0)
 
 
 def swapped(value, axis, distance):
@@ -60,7 +65,7 @@
 
 
 def blk_total(value):
-    return lax.psum(value, "blk")
+    return add_all(value, "blk")
 
 
 def row_mask(start, count, limit):

time: 478 us -> 540 us (1.13)
  matrix products: 117 us -> 142 us
  other arithmetic: 19.3 us -> 42 us
  local copies, waits for them, and re-layouts: 22.2 us -> 43.4 us
  blocking collectives: 27.4 us -> 8.31 us
  waiting for transfers between devices: 253 us -> 262 us
    all_gather x0 -> x4, waiting for transfers between devices: none -> 148 us  [add_all(): parts = lax.all_gather(value, mesh_axis)]
    psum x3 -> x0, waiting for transfers between devices: 141 us -> none  [blk_total(): return lax.psum(value, 'blk')]
    psum x2 -> x0, blocking collectives: 27.4 us -> none  [blk_total(): return lax.psum(value, 'blk')]
    reduce_sum x0 -> x5, other arithmetic: none -> 20.7 us  [add_all(): return jnp.sum(parts, axis=0)]
    all_gather x0 -> x2, local copies, waits for them, and re-layouts: none -> 17.2 us  [add_all(): parts = lax.all_gather(value, mesh_axis)]
    dot_general x5, matrix products: 23.4 us -> 34.7 us  [complex_apply_t(): lax.dot_general(matrix[1], rotate_parts(vec), dims, preferred_element_typ...]
    dot_general x5, matrix products: 26.3 us -> 34.8 us  [complex_apply_t(): lax.dot_general(matrix[0], vec, dims, preferred_element_type=jnp.float32)]
    all_gather x0 -> x1, blocking collectives: none -> 8.31 us  [add_all(): parts = lax.all_gather(value, mesh_axis)]
  transfers between devices with their start and end apart: 14 -> 15, of which waited for: 12 -> 14; matrix products, arithmetic and copies ran while one was open for 10% -> 11% of each run, Pallas kernels for 0% -> 0%
where the time goes in v1:
time: 540 us; the launch traced here: 531 us
  waiting for transfers between devices  262 us (49%)
  matrix products  142 us (26%)
  local copies, waits for them, and re-layouts  43.4 us (8%)
  other arithmetic  42 us (8%)
  starting transfers between devices  16.8 us (3%)
  between operations  16.7 us (3%)
  blocking collectives  8.31 us (2%)
    all_gather x4, waiting for transfers between devices, add_all(): parts = lax.all_gather(value, mesh_axis)  148 us
    psum x1, waiting for transfers between devices, per_device(): total = lax.psum(complex_apply_t(pivot_root, solved_root), 'cube')  64.2 us
    ppermute x10, waiting for transfers between devices, swapped(): lax.ppermute(value, axis, [(i, i ^ 1 << distance) for i in range(lax.axis...  50.2 us
    dot_general x5, matrix products, complex_apply(): first = jnp.dot(matrix[0], vec, preferred_element_type=jnp.float32)  35.8 us
    dot_general x5, matrix products, complex_apply_t(): lax.dot_general(matrix[0], vec, dims, preferred_element_type=jnp.float32)  34.8 us
    dot_general x5, matrix products, complex_apply_t(): lax.dot_general(matrix[1], rotate_parts(vec), dims, preferred_element_typ...  34.7 us
    dot_general x5, matrix products, complex_apply(): jnp.dot(matrix[1], rotate_parts(vec), preferred_element_type=jnp.float32)  32.9 us
    reduce_sum x5, other arithmetic, add_all(): return jnp.sum(parts, axis=0)  20.7 us
  transfers between devices with their start and end apart: 15, of which 14 were waited for; matrix products, arithmetic and copies ran while one was open for 11% of the time, Pallas kernels for 0%

profile of v1, /device:TPU:0, one launch (start us, length us, event | category | flops | bytes accessed | tf_op | source)
XLA Modules:
  0.0 531.1 jit_solution(1609403822463187938)
XLA Ops:
  12.8 15.5 %fusion.2 = f32[128,5120]{1,0:T(8,128)} fusion(bf16[2,5120,2560]{2,1,0:T(8,128)(2,1)} %param.15, bf16[2560,64]{1,0:T(8,128)(2,1)S(1)} %get-tuple-element.24, bf16[2560,64]{1,0:T(8,128)(2,1)S(1)} %get-tuple-element.23), kind=kOutput, calls=%fused_computation.4 | convolution fusion | flops 3356753920 | bytes 29491200 | tf_op jit(solution)/shard_map/dot_general | solution.py:26
  28.3 15.2 %fusion.35 = f32[5120,128]{0,1:T(8,128)S(1)} fusion(f32[128,5120]{1,0:T(8,128)} %fusion.2, bf16[2,5120,2560]{2,1,0:T(8,128)(2,1)} %param.15, f32[2560]{0:T(1024)S(1)} %get-tuple-element.43, bf16[4,2560,128]{2,1,0:T(8,128)(2,1)} %param.12, s32[]{:T(128)S(6)} %select_n.231), kind=kOutput, calls=%fused_computation.35 | convolution fusion | flops 3357081600 | bytes 32122884 | tf_op jit(solution)/shard_map/dot_general | solution.py:25
  53.7 79.6 %all-gather.10.cloned.1.call-done = f32[23040,128]{0,1:T(8,128)} async-done(((f32[5760,128]{0,1:T(8,128)}), f32[23040,128]{0,1:T(8,128)}) %all-gather.10.cloned.1.call-update) | async-done | bytes 11796496 | tf_op jit(solution)/shard_map/all_gather | solution.py:11
  133.3 13.2 %reshape.408 = f32[4,5760,128]{1,0,2:T(4,128)} reshape(f32[23040,128]{0,1:T(8,128)} %all-gather.10.cloned.1.call-done) | data formatting | bytes 23592960 | tf_op jit(solution)/shard_map/all_gather | solution.py:11
  146.5 9.8 %reduce_sum.63 = f32[5760,128]{0,1:T(8,128)S(1)} reduce(f32[4,5760,128]{1,0,2:T(4,128)} %reshape.408, f32[]{:T(128)} %constant.135.clone.1), dimensions={0}, to_apply=%region_0.1 | reduce | flops 2211840 | bytes 14745604 | tf_op jit(solution)/shard_map/reduce_sum | solution.py:12
  158.2 4.7 collective-permute-done
  165.7 6.3 %collective-permute-done.1 = bf16[1280,128]{1,0:T(8,128)(2,1)S(1)} collective-permute-done((bf16[1280,128]{1,0:T(8,128)(2,1)S(1)}, bf16[1280,128]{1,0:T(8,128)(2,1)S(1)}, u32[]{:S(2)}, u32[]{:S(2)}) %collective-permute-start.1) | collective-permute-done | bytes 327712 | tf_op jit(solution)/shard_map/ppermute | solution.py:16
  175.7 8.1 %fusion.14 = f32[128,2560]{1,0:T(8,128)S(1)} fusion(bf16[2,2560,2560]{2,1,0:T(8,128)(2,1)} %param.14, bf16[2560,64]{1,0:T(8,128)(2,1)S(1)} %get-tuple-element.22, bf16[2560,64]{1,0:T(8,128)(2,1)S(1)} %get-tuple-element.21), kind=kOutput, calls=%fused_computation.16 | convolution fusion | flops 1679032320 | bytes 15073280 | tf_op jit(solution)/shard_map/dot_general | solution.py:26
  184.5 10.2 %fusion.58 = f32[2560,128]{0,1:T(8,128)} fusion(f32[128,2560]{1,0:T(8,128)S(1)} %fusion.14, bf16[2560,128]{1,0:T(8,128)(2,1)S(1)} %bitcast.171, bf16[2,2560,2560]{2,1,0:T(8,128)(2,1)} %param.14), kind=kOutput, calls=%fused_computation.50 | convolution fusion | flops 1678049280 | bytes 16384000 | tf_op jit(solution)/shard_map/dot_general | solution.py:25
  201.2 44.0 %all-gather.12.cloned.1.call-done = f32[11520,128]{1,0:T(8,128)} async-done(((f32[2880,128]{1,0:T(8,128)}), f32[11520,128]{1,0:T(8,128)}) %all-gather.12.cloned.1.call-update) | async-done | bytes 5898256 | tf_op jit(solution)/shard_map/all_gather | solution.py:11
  245.3 4.3 reduce_sum.64
  268.0 9.0 %collective-permute-done.4 = bf16[1280,128]{1,0:T(8,128)(2,1)} collective-permute-done((bf16[1280,128]{1,0:T(8,128)(2,1)S(1)}, bf16[1280,128]{1,0:T(8,128)(2,1)}, u32[]{:S(2)}, u32[]{:S(2)}) %collective-permute-start.4) | collective-permute-done | bytes 327712 | tf_op jit(solution)/shard_map/ppermute | solution.py:16
  286.5 5.0 fusion.26
  291.6 6.0 %fusion.79 = f32[1280,128]{0,1:T(8,128)} fusion(f32[128,1280]{1,0:T(8,128)S(1)} %fusion.26, bf16[2560,128]{1,0:T(8,128)(2,1)S(1)} %bitcast.173, bf16[2,1280,2560]{2,1,0:T(8,128)(2,1)} %param.13), kind=kOutput, calls=%fused_computation.67 | convolution fusion | flops 839024640 | bytes 8519680 | tf_op jit(solution)/shard_map/dot_general | solution.py:25
  302.0 21.2 %all-gather.14.cloned.1.call-done = f32[5120,128]{0,1:T(8,128)} async-done(((f32[1280,128]{0,1:T(8,128)}), f32[5120,128]{0,1:T(8,128)}) %all-gather.14.cloned.1.call-update) | async-done | bytes 2621456 | tf_op jit(solution)/shard_map/all_gather | solution.py:11
  336.5 5.0 fusion.49
  341.9 9.1 %fusion.12 = f32[128,2560]{0,1:T(8,128)S(1)} fusion(bf16[2,2560,2560]{2,1,0:T(8,128)(2,1)} %param.14, bf16[2560,64]{1,0:T(8,128)(2,1)} %get-tuple-element.18, bf16[2560,64]{1,0:T(8,128)(2,1)} %get-tuple-element.17), kind=kOutput, calls=%fused_computation.14 | convolution fusion | flops 1679032320 | bytes 15728640 | tf_op jit(solution)/shard_map/dot_general | solution.py:33
  351.0 10.0 %fusion.61 = f32[128,2560]{0,1:T(8,128)} fusion(f32[128,2560]{0,1:T(8,128)S(1)} %fusion.12, bf16[2560,128]{1,0:T(8,128)(2,1)S(1)} %copy-done.2, bf16[2,2560,2560]{2,1,0:T(8,128)(2,1)} %param.14), kind=kOutput, calls=%fused_computation.51 | convolution fusion | flops 1678049280 | bytes 16384000 | tf_op jit(solution)/shard_map/dot_general | solution.py:32
  361.0 64.2 %all-reduce.2.cloned.1.call-done = f32[2560,128]{0,1:T(8,128)} async-done(((f32[2560,128]{0,1:T(8,128)}), f32[2560,128]{0,1:T(8,128)}) %all-reduce.2.cloned.1.call-update) | async-done | bytes 1310736 | tf_op jit(solution)/shard_map/psum | solution.py:173
  432.1 8.3 %all_gather.32 = f32[4,320,128]{2,1,0:T(8,128)} all-gather(f32[1,320,128]{2,1,0:T(8,128)S(1)} %convert_select_fusion.1), channel_id=1, replica_groups=mesh['cube'=8,'blk'=4] {'blk'}, dimensions={0}, use_global_device_ids=true | all-gather | bytes 819200 | tf_op jit(solution)/shard_map/all_gather | solution.py:11
  447.8 8.7 %collective-permute-done.5 = bf16[1280,128]{1,0:T(8,128)(2,1)S(1)} collective-permute-done((bf16[1280,128]{1,0:T(8,128)(2,1)S(1)}, bf16[1280,128]{1,0:T(8,128)(2,1)S(1)}, u32[]{:S(2)}, u32[]{:S(2)}) %collective-permute-start.5) | collective-permute-done | bytes 327712 | tf_op jit(solution)/shard_map/ppermute | solution.py:16
  469.2 16.1 %fusion = f32[128,2560]{0,1:T(8,128)} fusion(bf16[2,5120,2560]{2,1,0:T(8,128)(2,1)} %param.15, bf16[5120,64]{0,1:T(8,128)(2,1)S(1)} %get-tuple-element.16, bf16[5120,64]{0,1:T(8,128)(2,1)S(1)} %get-tuple-element.15), kind=kOutput, calls=%fused_computation.2 | convolution fusion | flops 3358064640 | bytes 28835840 | tf_op jit(solution)/shard_map/dot_general | solution.py:33
  488.4 14.0 %fusion.52 = f32[128,2560]{0,1:T(8,128)} fusion(f32[128,2560]{0,1:T(8,128)} %fusion, bf16[5120,128]{0,1:T(8,128)(2,1)S(1)} %copy-done.4, bf16[2,5120,2560]{2,1,0:T(8,128)(2,1)} %param.15), kind=kOutput, calls=%fused_computation.48 | convolution fusion | flops 3355770880 | bytes 30146560 | tf_op jit(solution)/shard_map/dot_general | solution.py:32
  516.8 6.6 %collective-permute-done.9 = bf16[1280,128]{1,0:T(8,128)(2,1)S(1)} collective-permute-done((bf16[1280,128]{1,0:T(8,128)(2,1)S(1)}, bf16[1280,128]{1,0:T(8,128)(2,1)S(1)}, u32[]{:S(2)}, u32[]{:S(2)}) %collective-permute-start.9) | collective-permute-done | bytes 327712 | tf_op jit(solution)/shard_map/ppermute | solution.py:16
  (147 shorter events, 120.3 us)
Async XLA Ops:
  7.2 126.1 %all-gather.10.cloned.1.call-start = ((), (), s32[]{:S(2)}) async-start(), calls=%async_computation.2 | async-start | bytes 14745600 | tf_op jit(solution)/shard_map/all_gather | solution.py:11
  52.8 192.5 %all-gather.12.cloned.1.call-start = ((), (), s32[]{:S(2)}) async-start(), calls=%async_computation.3 | async-start | bytes 7372800 | tf_op jit(solution)/shard_map/all_gather | solution.py:11
  156.5 6.4 %collective-permute-start = (bf16[640,128]{1,0:T(8,128)(2,1)S(1)}, bf16[640,128]{1,0:T(8,128)(2,1)S(1)}, u32[]{:S(2)}, u32[]{:S(2)}) collective-permute-start(bf16[640,128]{1,0:T(8,128)(2,1)S(1)} %copy.146), channel_id=1, source_target_pairs={{0,4},{4,0},{8,12},{12,8},{16,20},{20,16},{24,28},{28,24},{1,5},{5... | collective-permute-start | bytes 491528 | tf_op jit(solution)/shard_map/ppermute | solution.py:16
  163.0 9.1 %collective-permute-start.1 = (bf16[1280,128]{1,0:T(8,128)(2,1)S(1)}, bf16[1280,128]{1,0:T(8,128)(2,1)S(1)}, u32[]{:S(2)}, u32[]{:S(2)}) collective-permute-start(bf16[1280,128]{1,0:T(8,128)(2,1)S(1)} %maximum_select_fusion.3), channel_id=1, source_target_pairs={{0,8},{4,12},{8,0},{12,4},{16,24},{20,28},{24,16},{28,20},{1,9},{5... | collective-permute-start | bytes 983048 | tf_op jit(solution)/shard_map/ppermute | solution.py:16
  175.7 8.1 %copy-start.5 = (bf16[2,320,2560]{2,1,0:T(8,128)(2,1)S(1)}, bf16[2,320,2560]{2,1,0:T(8,128)(2,1)}, u32[]{:S(2)}) copy-start(bf16[2,320,2560]{2,1,0:T(8,128)(2,1)} %param.16) | copy-start | bytes 9830404
  201.0 122.3 %all-gather.14.cloned.1.call-start = ((), (), s32[]{:S(2)}) async-start(), calls=%async_computation.4 | async-start | bytes 3276800 | tf_op jit(solution)/shard_map/all_gather | solution.py:11
  250.4 4.7 collective-permute-start.2
  255.2 5.6 %collective-permute-start.3 = (bf16[640,128]{1,0:T(8,128)(2,1)S(1)}, bf16[640,128]{1,0:T(8,128)(2,1)S(1)}, u32[]{:S(2)}, u32[]{:S(2)}) collective-permute-start(bf16[640,128]{1,0:T(8,128)(2,1)S(1)} %maximum_select_fusion.6), channel_id=1, source_target_pairs={{0,8},{4,12},{8,0},{12,4},{16,24},{20,28},{24,16},{28,20},{1,9},{5... | collective-permute-start | bytes 491528 | tf_op jit(solution)/shard_map/ppermute | solution.py:16
  260.8 16.2 %collective-permute-start.4 = (bf16[1280,128]{1,0:T(8,128)(2,1)S(1)}, bf16[1280,128]{1,0:T(8,128)(2,1)}, u32[]{:S(2)}, u32[]{:S(2)}) collective-permute-start(bf16[1280,128]{1,0:T(8,128)(2,1)S(1)} %maximum_select_fusion.4), channel_id=1, source_target_pairs={{0,16},{4,20},{8,24},{12,28},{16,0},{20,4},{24,8},{28,12},{1,17},{... | collective-permute-start | bytes 983048 | tf_op jit(solution)/shard_map/ppermute | solution.py:16
  268.0 10.3 %copy-start = (f32[1,2560,128]{2,1,0:T(8,128)S(1)}, f32[1,2560,128]{2,1,0:T(8,128)}, u32[]{:S(2)}) copy-start(f32[1,2560,128]{2,1,0:T(8,128)} %copy.114) | copy-start | bytes 3932164
  284.6 1.8 copy-start.7
  297.6 127.6 %all-reduce.2.cloned.1.call-start = ((), (), s32[]{:S(2)}) async-start(), calls=%async_computation | async-start | bytes 2621440 | tf_op jit(solution)/shard_map/psum | solution.py:173
  341.4 163.8 %all-gather.8.cloned.1.call-start = ((), (), s32[]{:S(2)}) async-start(), calls=%async_computation.1 | async-start | bytes 1638400 | tf_op jit(solution)/shard_map/all_gather | solution.py:11
  341.9 9.1 %copy-start.2 = (bf16[2560,128]{1,0:T(8,128)(2,1)S(1)}, bf16[2560,128]{1,0:T(8,128)(2,1)}, u32[]{:S(2)}) copy-start(bf16[2560,128]{1,0:T(8,128)(2,1)} %copy-done.1) | copy-start | bytes 1966084
  441.5 2.6 copy-start.6
  446.5 10.0 %collective-permute-start.5 = (bf16[1280,128]{1,0:T(8,128)(2,1)S(1)}, bf16[1280,128]{1,0:T(8,128)(2,1)S(1)}, u32[]{:S(2)}, u32[]{:S(2)}) collective-permute-start(bf16[1280,128]{1,0:T(8,128)(2,1)S(1)} %select_convert_fusion.1), channel_id=1, source_target_pairs={{0,8},{4,12},{8,0},{12,4},{16,24},{20,28},{24,16},{28,20},{1,9},{5... | collective-permute-start | bytes 983048 | tf_op jit(solution)/shard_map/ppermute | solution.py:16
  456.6 5.7 %collective-permute-start.6 = (bf16[640,128]{1,0:T(8,128)(2,1)S(1)}, bf16[640,128]{1,0:T(8,128)(2,1)S(1)}, u32[]{:S(2)}, u32[]{:S(2)}) collective-permute-start(bf16[640,128]{1,0:T(8,128)(2,1)S(1)} %select_convert_fusion.2), channel_id=1, source_target_pairs={{0,4},{4,0},{8,12},{12,8},{16,20},{20,16},{24,28},{28,24},{1,5},{5... | collective-permute-start | bytes 491528 | tf_op jit(solution)/shard_map/ppermute | solution.py:16
  458.4 5.7 %copy-start.3 = (bf16[5120,128]{0,1:T(8,128)(2,1)}, bf16[5120,128]{0,1:T(8,128)(2,1)S(1)}, u32[]{:S(2)}) copy-start(bf16[5120,128]{0,1:T(8,128)(2,1)S(1)} %fusion.75) | copy-start | bytes 3932164
  462.5 5.5 %copy-start.12 = (bf16[640,128]{1,0:T(8,128)(2,1)}, bf16[640,128]{1,0:T(8,128)(2,1)S(1)}, u32[]{:S(2)}) copy-start(bf16[640,128]{1,0:T(8,128)(2,1)S(1)} %multiply_convert_fusion.3) | copy-start | bytes 491524
  462.5 5.4 %collective-permute-start.7 = (bf16[640,128]{1,0:T(8,128)(2,1)S(1)}, bf16[640,128]{1,0:T(8,128)(2,1)S(1)}, u32[]{:S(2)}, u32[]{:S(2)}) collective-permute-start(bf16[640,128]{1,0:T(8,128)(2,1)S(1)} %multiply_convert_fusion.3), channel_id=1, source_target_pairs={{0,4},{4,0},{8,12},{12,8},{16,20},{20,16},{24,28},{28,24},{1,5},{5... | collective-permute-start | bytes 491528 | tf_op jit(solution)/shard_map/ppermute | solution.py:16
  468.0 17.4 %collective-permute-start.8 = (bf16[1280,128]{1,0:T(8,128)(2,1)S(1)}, bf16[1280,128]{1,0:T(8,128)(2,1)S(1)}, u32[]{:S(2)}, u32[]{:S(2)}) collective-permute-start(bf16[1280,128]{1,0:T(8,128)(2,1)S(1)} %maximum_select_fusion.5), channel_id=1, source_target_pairs={{0,8},{4,12},{8,0},{12,4},{16,24},{20,28},{24,16},{28,20},{1,9},{5... | collective-permute-start | bytes 983048 | tf_op jit(solution)/shard_map/ppermute | solution.py:16
  485.5 2.9 copy-start.4
  506.6 3.5 copy-start.8
  513.5 9.9 %collective-permute-start.9 = (bf16[1280,128]{1,0:T(8,128)(2,1)S(1)}, bf16[1280,128]{1,0:T(8,128)(2,1)S(1)}, u32[]{:S(2)}, u32[]{:S(2)}) collective-permute-start(bf16[1280,128]{1,0:T(8,128)(2,1)S(1)} %select_convert_fusion), channel_id=1, source_target_pairs={{0,4},{4,0},{8,12},{12,8},{16,20},{20,16},{24,28},{28,24},{1,5},{5... | collective-permute-start | bytes 983048 | tf_op jit(solution)/shard_map/ppermute | solution.py:16
  (5 other events, 5.0 us)
Sparse Core Ops, SparseCore 0:
  52.9 80.3 all-gather.9
  201.1 44.1 all-gather.11
  297.7 25.4 all-gather.13
  341.6 83.6 all-reduce.1
  488.5 16.6 all-gather.7
